TPU v7x, 32 devices: a whole 2x2x4 slice. The times are simulated.
32 devices in a mesh: dp: 8 (over y, x, core), mp: 4 (over z).
Axes of the slice: x: 2, y: 2, z: 4, core: 2. Of those that a mesh axis runs over, the one named last changes fastest.
Arguments:
- tokens: bfloat16 [320, 4096], P('dp'), may hold values from -6 to 6
- attn_gain: float32 [4096], replicated, may hold values from 0.1 to 1.9
- head_gain: float32 [4096], replicated, may hold values from 0.1 to 1.9
- qkv_weight: bfloat16 [4096, 3, 4096], P('dp', None, 'mp'), may hold values from -0.09375 to 0.09375
- out_weight: bfloat16 [4096, 4096], P('mp', 'dp'), may hold values from -0.09375 to 0.09375
- head_weight: bfloat16 [4096, 1024], P('mp'), may hold values from -0.09375 to 0.09375
- key_cache: bfloat16 [320, 64, 4096], P('dp', None, 'mp'), may hold values from -400 to 400
- value_cache: bfloat16 [320, 64, 4096], P('dp', None, 'mp'), may hold values from -6 to 6
- parents: int32 [320], P('dp'), may hold values from 0 to 19
- allowed: int32 [320, 2], P('dp'), may hold values from 0 to 7, all different within a row
Outputs:
- new_stream: bfloat16 [320, 4096], P('dp')
- next_logits: float32 [320, 256], P('dp', 'mp')
Inputs may be any that keep to these rules, and one draw needn't show every extreme that they name: `parents`: a beam's parent is a beam of the same query. `allowed`: the 2 block ids of a beam differ.
All inputs are finite; a program needn't handle non-finite values.
Results may differ from a plain program's by a relative error of at most 0.017.
Values may be sent and summed in bfloat16 or wider, within the bound.
No kernel may reach another device: no remote copies, remote signals or barrier semaphores. Data moves between devices by JAX's collectives and lax.ppermute only.
A program may use at most 128 MiB of HBM per device.

v0:
```python
import jax
import jax.numpy as jnp
from jax import lax
from jax.sharding import PartitionSpec as P

HEAD = 128
BEAMS = 20
BLOCK = 128


def root_norm(values, gain_vec):
    float_values = values.astype(jnp.float32)
    factor = lax.rsqrt(jnp.mean(float_values * float_values, axis=-1, keepdims=True) + 1e-06)
    return float_values * factor * gain_vec


def select_blocks(whole_logits, allowed):
    block_count = whole_logits.shape[1] // BLOCK
    block_list = whole_logits.reshape(whole_logits.shape[0], block_count, BLOCK)
    one_hot_rows = (
        allowed[:, :, None] == jnp.arange(block_count, dtype=jnp.int32)[None, None, :]
    ).astype(jnp.float32)
    selected_token = jnp.einsum(
        "ioh,ihp->iop", one_hot_rows, block_list, precision=lax.Precision.HIGHEST
    )
    return selected_token.reshape(whole_logits.shape[0], -1)


def on_device(
    tokens,
    attn_gain,
    head_gain,
    qkv_weight,
    out_weight,
    head_weight,
    key_cache,
    value_cache,
    parents,
    allowed,
):
    row_count = tokens.shape[0]
    normed = root_norm(tokens, attn_gain).astype(jnp.bfloat16)
    spread = lax.all_to_all(normed, "dp", split_axis=1, concat_axis=0, tiled=True)
    depth_part = qkv_weight.shape[0]
    head_width = qkv_weight.shape[2]
    flat_qkv = qkv_weight.reshape(depth_part, 3 * head_width)
    projected = lax.psum_scatter(
        jnp.dot(spread, flat_qkv, preferred_element_type=jnp.float32),
        "dp",
        scatter_dimension=0,
        tiled=True,
    )
    projected = projected.astype(jnp.bfloat16).reshape(row_count, 3, head_width)
    local_heads = head_width // HEAD
    length = key_cache.shape[1] + 1
    source = jnp.arange(row_count, dtype=jnp.int32) // BEAMS * BEAMS + parents
    key_rows = jnp.concatenate(
        [jnp.take(key_cache, source, axis=0), projected[:, 1][:, None]], axis=1
    )
    value_rows = jnp.concatenate(
        [jnp.take(value_cache, source, axis=0), projected[:, 2][:, None]], axis=1
    )
    key_rows = key_rows.reshape(row_count, length, local_heads, HEAD)
    value_rows = value_rows.reshape(row_count, length, local_heads, HEAD)
    queries = projected[:, 0].reshape(row_count, local_heads, HEAD)
    scores = jnp.einsum(
        "thd,tjhd->thj", queries, key_rows, preferred_element_type=jnp.float32
    ) * HEAD ** (-0.5)
    softmax_w = jax.nn.softmax(scores, axis=-1).astype(jnp.bfloat16)
    attention_result = jnp.einsum(
        "thj,tjhd->thd", softmax_w, value_rows, preferred_element_type=jnp.float32
    )
    attention_result = attention_result.astype(jnp.bfloat16).reshape(row_count, head_width)
    partial_value = jnp.dot(
        attention_result,
        lax.all_gather(out_weight, "dp", axis=1, tiled=True),
        preferred_element_type=jnp.float32,
    )
    attn_out = lax.psum(partial_value, "mp")
    stream = tokens.astype(jnp.float32) + attn_out
    head_input = root_norm(stream, head_gain).astype(jnp.bfloat16)
    depth_rows = head_weight.shape[0]
    own_part = lax.dynamic_slice_in_dim(
        head_input, lax.axis_index("mp") * depth_rows, depth_rows, 1
    )
    partial_logits = jnp.dot(own_part, head_weight, preferred_element_type=jnp.float32)
    next_logits = lax.psum_scatter(
        select_blocks(partial_logits, allowed).astype(jnp.bfloat16),
        "mp",
        scatter_dimension=1,
        tiled=True,
    ).astype(jnp.float32)
    return (stream.astype(jnp.bfloat16), next_logits)


def solution(mesh):
    in_specs = (
        P("dp", None),
        P(),
        P(),
        P("dp", None, "mp"),
        P("mp", "dp"),
        P("mp", None),
        P("dp", None, "mp"),
        P("dp", None, "mp"),
        P("dp"),
        P("dp", None),
    )
    out_specs = (P("dp", None), P("dp", "mp"))
    return jax.shard_map(
        on_device, mesh=mesh, in_specs=in_specs, out_specs=out_specs, check_vma=False
    )
```

profile of v0, /device:TPU:0, one launch (start us, length us, event | category | flops | bytes accessed | tf_op | source)
XLA Modules:
  0.0 211.9 jit_solution(16103499963755374255)
XLA Ops:
  7.2 0.0 copy-start
  7.2 1.3 fusion.11
  8.5 1.1 fusion.13
  9.6 0.7 copy.55
  10.4 5.2 %all-to-all-start = ((bf16[40,8,512]{2,0,1:T(8,128)(2,1)}), bf16[40,8,512]{2,0,1:T(8,128)(2,1)S(1)}, u32[]{:S(2)}, u32[]{:S(2)}) async-start(bf16[40,8,512]{2,0,1:T(8,128)(2,1)} %bitcast.32), calls=%async_computation | async-start | bytes 655360 | tf_op jit(solution)/shard_map/all_to_all | solution.py:43
  15.6 0.0 reduce-scatter.5.cloned.1.call-start
  15.6 4.7 %copy.24 = bf16[512,3,1024]{0,2,1:T(8,128)(2,1)} copy(bf16[512,3,1024]{2,0,1:T(8,128)(2,1)} %param.15) | data formatting | bytes 6291456 | tf_op args[3]
  20.3 2.9 %all-to-all-done = bf16[40,8,512]{2,0,1:T(8,128)(2,1)S(1)} async-done(((bf16[40,8,512]{2,0,1:T(8,128)(2,1)}), bf16[40,8,512]{2,0,1:T(8,128)(2,1)S(1)}, u32[]{:S(2)}, u32[]{:S(2)}) %all-to-all-start) | async-done | bytes 327712 | tf_op jit(solution)/shard_map/all_to_all | solution.py:43
  23.2 0.0 copy-start.3
  23.2 5.0 %fusion.35 = f32[320,3072]{1,0:T(8,128)} fusion(bf16[320,512]{1,0:T(8,128)(2,1)S(1)} %bitcast.34, bf16[512,3072]{0,1:T(8,128)(2,1)} %bitcast.33), kind=kOutput, calls=%fused_computation.57 | convolution fusion | flops 1006632960 | bytes 7405568 | tf_op jit(solution)/shard_map/dot_general | solution.py:48
  28.2 0.0 reduce-scatter.5.cloned.1.call-update
  28.2 0.0 all-gather.2.cloned.1.call-start
  28.3 0.7 all-gather.2.cloned.1.call-update
  29.0 0.0 all-reduce.2.cloned.1.call-start
  29.0 0.0 copy-done.3
  29.1 7.2 %gather_fusion = bf16[40,64,1024]{2,1,0:T(8,128)(2,1)} fusion(bf16[40,64,1024]{2,1,0:T(8,128)(2,1)} %param.18, s32[1024]{0:T(1024)S(1)} %pad_clamp_fusion), kind=kCustom, calls=%fused_computation.clone | custom fusion | bytes 10485920 | tf_op jit(solution)/shard_map/jit(_take)/gather | solution.py:58
  36.3 7.6 %gather_fusion.1 = bf16[40,64,1024]{2,1,0:T(8,128)(2,1)} fusion(bf16[40,64,1024]{2,1,0:T(8,128)(2,1)} %param.19, s32[1024]{0:T(1024)S(1)} %pad_clamp_fusion), kind=kCustom, calls=%fused_computation.1.clone | custom fusion | bytes 10485920 | tf_op jit(solution)/shard_map/jit(_take)/gather | solution.py:61
  43.9 9.1 %broadcast_select_fusion.1 = (bf16[40,64,1024]{2,1,0:T(8,128)(2,1)}, bf16[40,64,1024]{2,1,0:T(8,128)(2,1)}) fusion(bf16[40,64,1024]{2,1,0:T(8,128)(2,1)} %gather_fusion, pred[40]{0:T(512)(128)(4,1)S(1)} %get-tuple-element.5, bf16[40,64,1024]{2,1,0:T(8,128)(2,1)} %gather_fusion.1), kind=kLoop, calls=%fused_computation.11 | loop fusion | flops 5242880 | bytes 20971560 | tf_op jit(solution)/shard_map/jit(_take)/select_n | solution.py:58
  52.9 24.6 %reduce-scatter.5.cloned.1.call-done = f32[40,3072]{1,0:T(8,128)} async-done(((f32[320,3072]{1,0:T(8,128)}), f32[40,3072]{1,0:T(8,128)}) %reduce-scatter.5.cloned.1.call-update) | async-done | bytes 491536 | tf_op jit(solution)/shard_map/reduce_scatter | solution.py:47
  77.6 1.1 convert_element_type.34
  78.6 0.4 reshape.54
  79.0 0.3 fusion.32
  79.3 11.1 %pad_maximum_fusion = (bf16[40,65,1024]{2,1,0:T(8,128)(2,1)}, bf16[40,65,1024]{2,1,0:T(8,128)(2,1)}) fusion(bf16[40,1,1024]{2,1,0:T(2,128)(2,1)S(1)} %get-tuple-element.7, bf16[40,64,1024]{2,1,0:T(8,128)(2,1)} %get-tuple-element.9, bf16[40,1,1024]{2,1,0:T(2,128)(2,1)S(1)} %get-tuple-element.8, bf16[40,64,1024]{2,1,0:T(8,128)(2,1)} %get-tuple-element.10), kind=kLoop, calls=%fused_computation.4 | loop fusion | flops 21299200 | bytes 21299200 | tf_op jit(solution)/shard_map/concatenate | solution.py:57
  90.4 9.1 %reshape.86 = bf16[40,65,8,128]{3,2,1,0:T(8,128)(2,1)} reshape(bf16[40,65,1024]{2,1,0:T(8,128)(2,1)} %get-tuple-element.11) | data formatting | bytes 10649600 | tf_op jit(solution)/shard_map/reshape | solution.py:63
  99.5 9.3 %reshape.87 = bf16[40,65,8,128]{3,2,1,0:T(8,128)(2,1)} reshape(bf16[40,65,1024]{2,1,0:T(8,128)(2,1)} %get-tuple-element.12) | data formatting | bytes 10649600 | tf_op jit(solution)/shard_map/reshape | solution.py:64
  108.8 5.9 %fusion.4 = f32[40,8,1,65]{3,2,1,0:T(1,128)S(1)} fusion(bf16[40,65,8,128]{3,2,1,0:T(8,128)(2,1)} %reshape.86, bf16[40,3,1024]{2,1,0:T(4,128)(2,1)S(1)} %reshape.54), kind=kOutput, calls=%fused_computation.8 | convolution fusion | flops 5324800 | bytes 5571840 | tf_op jit(solution)/shard_map/thd,tjhd->thj/dot_general | solution.py:66
  114.6 0.2 fusion.10
  114.9 4.2 %fusion.2 = f32[40,8,1,128]{3,2,1,0:T(1,128)S(1)} fusion(bf16[40,65,8,128]{3,2,1,0:T(8,128)(2,1)} %reshape.87, bf16[40,8,65,1]{2,1,0,3:T(8,128)(2,1)S(1)} %fusion.10), kind=kOutput, calls=%fused_computation.6 | convolution fusion | flops 5324800 | bytes 5530240 | tf_op jit(solution)/shard_map/thj,tjhd->thd/dot_general | solution.py:70
  119.1 16.2 %all-gather.2.cloned.1.call-done = bf16[1024,4096]{1,0:T(8,128)(2,1)} async-done(((bf16[1024,512]{1,0:T(8,128)(2,1)}), bf16[1024,4096]{1,0:T(8,128)(2,1)}) %all-gather.2.cloned.1.call-update) | async-done | bytes 8388624 | tf_op jit(solution)/shard_map/all_gather | solution.py:76
  135.3 0.0 copy-start.2
  135.3 5.9 %fusion.19 = f32[40,4096]{1,0:T(8,128)} fusion(bf16[1024,4096]{1,0:T(8,128)(2,1)} %all-gather.2.cloned.1.call-done, bf16[5,8,8,128]{3,2,1,0:T(8,128)(2,1)S(1)} %bitcast.36), kind=kOutput, calls=%fused_computation.34 | convolution fusion | flops 335544320 | bytes 9125888 | tf_op jit(solution)/shard_map/dot_general | solution.py:74
  141.2 0.0 all-reduce.2.cloned.1.call-update
  141.2 0.0 reduce-scatter.7.cloned.1.call-start
  141.3 0.0 copy-done.2
  141.3 0.1 copy.27
  141.4 0.7 dynamic-slice
  142.1 39.9 %all-reduce.2.cloned.1.call-done = f32[40,4096]{1,0:T(8,128)} async-done(((f32[40,4096]{1,0:T(8,128)}), f32[40,4096]{1,0:T(8,128)}) %all-reduce.2.cloned.1.call-update) | async-done | bytes 655376 | tf_op jit(solution)/shard_map/psum | solution.py:79
  181.9 0.0 copy-done.1
  181.9 1.3 multiply_reduce_fusion
  183.2 0.0 copy-done
  183.2 0.5 convolution_bitcast_fusion
  183.8 0.3 convolution_convert_fusion
  184.1 0.7 copy.40
  184.9 0.0 reduce-scatter.7.cloned.1.call-update
  184.9 0.8 convert_element_type.37
  185.7 18.2 %reduce-scatter.7.cloned.1.call-done = bf16[64,40]{1,0:T(8,128)(2,1)} async-done(((bf16[256,40]{1,0:T(8,128)(2,1)}), bf16[64,40]{1,0:T(8,128)(2,1)}) %reduce-scatter.7.cloned.1.call-update) | async-done | bytes 5136
  203.9 0.8 copy.39
  204.7 0.6 convert_element_type.41
  (7 shorter events, 0.1 us)
Async XLA Ops:
  7.2 176.1 %copy-start = (bf16[1024,1024]{1,0:T(8,128)(2,1)S(1)}, bf16[1024,1024]{1,0:T(8,128)(2,1)}, u32[]{:S(2)}) copy-start(bf16[1024,1024]{1,0:T(8,128)(2,1)} %param.17) | copy-start | bytes 6291460
  10.4 12.8 %all-to-all-start = ((bf16[40,8,512]{2,0,1:T(8,128)(2,1)}), bf16[40,8,512]{2,0,1:T(8,128)(2,1)S(1)}, u32[]{:S(2)}, u32[]{:S(2)}) async-start(bf16[40,8,512]{2,0,1:T(8,128)(2,1)} %bitcast.32), calls=%async_computation | async-start | bytes 655360 | tf_op jit(solution)/shard_map/all_to_all | solution.py:43
  15.6 62.0 %reduce-scatter.5.cloned.1.call-start = ((), (), s32[]{:S(2)}) async-start(), calls=%async_computation.3 | async-start | bytes 4423680 | tf_op jit(solution)/shard_map/reduce_scatter | solution.py:47
  23.2 5.8 %copy-start.3 = (s32[40]{0:T(128)S(1)}, s32[40]{0:T(128)}, u32[]{:S(2)}) copy-start(s32[40]{0:T(128)} %param.20) | copy-start | bytes 484
  28.2 107.1 %all-gather.2.cloned.1.call-start = ((), (), s32[]{:S(2)}) async-start(), calls=%async_computation.4 | async-start | bytes 9437184 | tf_op jit(solution)/shard_map/all_gather | solution.py:76
  29.0 153.0 %all-reduce.2.cloned.1.call-start = ((), (), s32[]{:S(2)}) async-start(), calls=%async_computation.5 | async-start | bytes 1310720 | tf_op jit(solution)/shard_map/psum | solution.py:79
  135.3 6.0 %copy-start.2 = (s32[40,2]{0,1:T(2,128)S(1)}, s32[40,2]{0,1:T(2,128)}, u32[]{:S(2)}) copy-start(s32[40,2]{0,1:T(2,128)} %param.21) | copy-start | bytes 964
  135.3 46.6 %copy-start.1 = (bf16[40,4096]{1,0:T(8,128)(2,1)S(1)}, bf16[40,4096]{1,0:T(8,128)(2,1)}, u32[]{:S(2)}) copy-start(bf16[40,4096]{1,0:T(8,128)(2,1)} %param.12) | copy-start | bytes 983044
  141.2 62.7 %reduce-scatter.7.cloned.1.call-start = ((), (), s32[]{:S(2)}) async-start(), calls=%async_computation.6 | async-start | bytes 81920
Sparse Core Ops, SparseCore 0:
  28.3 49.1 reduce-scatter.4
  79.4 55.8 all-gather.1
  141.4 40.5 all-reduce.1
  185.0 18.8 reduce-scatter.6
where the time goes:
time: 213 us; the launch traced here: 212 us
  waiting for transfers between devices  103 us (48%)
  local copies, waits for them, and re-layouts  41.6 us (20%)
  other arithmetic  26.6 us (12%)
  matrix products  21.8 us (10%)
  between operations  13.9 us (7%)
  starting transfers between devices  5.36 us (3%)
    psum x1, waiting for transfers between devices, on_device(): attn_out = lax.psum(partial_value, 'mp')  39.9 us
    reduce_scatter x1, waiting for transfers between devices, on_device(): lax.psum_scatter(jnp.dot(spread, flat_qkv, preferred_element_type=jnp.flo...  24.6 us
    unnamed x5, waiting for transfers between devices  19 us
    all_gather x1, waiting for transfers between devices, on_device(): lax.all_gather(out_weight, 'dp', axis=1, tiled=True)  16.2 us
    concatenate x1, other arithmetic, on_device(): jnp.concatenate([jnp.take(key_cache, source, axis=0), projected[:, 1][:,...  11.1 us
    reshape x1, local copies, waits for them, and re-layouts, on_device(): value_rows = value_rows.reshape(row_count, length, local_heads, HEAD)  9.25 us
    reshape x1, local copies, waits for them, and re-layouts, on_device(): key_rows = key_rows.reshape(row_count, length, local_heads, HEAD)  9.11 us
    select_n x1, other arithmetic, on_device(): jnp.take(key_cache, source, axis=0)  9.08 us
  transfers between devices with their start and end apart: 5, of which 5 were waited for; matrix products, arithmetic and copies ran while one was open for 34% of the time, Pallas kernels for 0%

commit v1 on v0

--- a/solution.py
+++ b/solution.py
@@ -6,6 +6,11 @@
 HEAD = 128
 BEAMS = 20
 BLOCK = 128
+
+
+def reach_racks(mat, mesh_name):
+    z2 = jnp.sum(lax.all_gather(mat, mesh_name), axis=0)
+    return z2
 
 
 def root_norm(values, gain_vec):
@@ -76,7 +81,7 @@
         lax.all_gather(out_weight, "dp", axis=1, tiled=True),
         preferred_element_type=jnp.float32,
     )
-    attn_out = lax.psum(partial_value, "mp")
+    attn_out = reach_racks(partial_value, "mp")
     stream = tokens.astype(jnp.float32) + attn_out
     head_input = root_norm(stream, head_gain).astype(jnp.bfloat16)
     depth_rows = head_weight.shape[0]

time: 213 us -> 229 us (1.075)
  waiting for transfers between devices: 103 us -> 116 us
  other arithmetic: 26.6 us -> 29.4 us
    all_gather x0 -> x1, waiting for transfers between devices: none -> 54.1 us  [reach_racks(): z2 = jnp.sum(lax.all_gather(mat, mesh_name), axis=0)]
    psum x1 -> x0, waiting for transfers between devices: 39.9 us -> none  [on_device(): attn_out = lax.psum(partial_value, 'mp')]
    reduce_sum x0 -> x1, other arithmetic: none -> 2.81 us  [reach_racks(): z2 = jnp.sum(lax.all_gather(mat, mesh_name), axis=0)]
  transfers between devices with their start and end apart: 5 -> 5, of which waited for: 5 -> 5; matrix products, arithmetic and copies ran while one was open for 34% -> 31% of each run, Pallas kernels for 0% -> 0%
where the time goes in v1:
time: 229 us; the launch traced here: 228 us
  waiting for transfers between devices  116 us (51%)
  local copies, waits for them, and re-layouts  41.6 us (18%)
  other arithmetic  29.4 us (13%)
  matrix products  21.8 us (10%)
  between operations  13.9 us (6%)
  starting transfers between devices  5.36 us (2%)
    all_gather x1, waiting for transfers between devices, reach_racks(): z2 = jnp.sum(lax.all_gather(mat, mesh_name), axis=0)  54.1 us
    reduce_scatter x1, waiting for transfers between devices, on_device(): lax.psum_scatter(jnp.dot(spread, flat_qkv, preferred_element_type=jnp.flo...  24.6 us
    unnamed x5, waiting for transfers between devices  18.2 us
    all_gather x1, waiting for transfers between devices, on_device(): lax.all_gather(out_weight, 'dp', axis=1, tiled=True)  16.2 us
    concatenate x1, other arithmetic, on_device(): jnp.concatenate([jnp.take(key_cache, source, axis=0), projected[:, 1][:,...  11.1 us
    reshape x1, local copies, waits for them, and re-layouts, on_device(): value_rows = value_rows.reshape(row_count, length, local_heads, HEAD)  9.25 us
    reshape x1, local copies, waits for them, and re-layouts, on_device(): key_rows = key_rows.reshape(row_count, length, local_heads, HEAD)  9.11 us
    select_n x1, other arithmetic, on_device(): jnp.take(key_cache, source, axis=0)  9.08 us
  transfers between devices with their start and end apart: 5, of which 5 were waited for; matrix products, arithmetic and copies ran while one was open for 31% of the time, Pallas kernels for 0%

profile of v1, /device:TPU:0, one launch (start us, length us, event | category | flops | bytes accessed | tf_op | source)
XLA Modules:
  0.0 228.1 jit_solution(9385093844057027077)
XLA Ops:
  7.2 0.0 copy-start
  7.2 1.3 fusion.11
  8.5 1.1 fusion.13
  9.6 0.7 copy.59
  10.4 5.2 %all-to-all-start = ((bf16[40,8,512]{2,0,1:T(8,128)(2,1)}), bf16[40,8,512]{2,0,1:T(8,128)(2,1)S(1)}, u32[]{:S(2)}, u32[]{:S(2)}) async-start(bf16[40,8,512]{2,0,1:T(8,128)(2,1)} %bitcast.33), calls=%async_computation | async-start | bytes 655360 | tf_op jit(solution)/shard_map/all_to_all | solution.py:48
  15.6 0.0 reduce-scatter.5.cloned.1.call-start
  15.6 4.7 %copy.28 = bf16[512,3,1024]{0,2,1:T(8,128)(2,1)} copy(bf16[512,3,1024]{2,0,1:T(8,128)(2,1)} %param.15) | data formatting | bytes 6291456 | tf_op args[3]
  20.3 2.9 %all-to-all-done = bf16[40,8,512]{2,0,1:T(8,128)(2,1)S(1)} async-done(((bf16[40,8,512]{2,0,1:T(8,128)(2,1)}), bf16[40,8,512]{2,0,1:T(8,128)(2,1)S(1)}, u32[]{:S(2)}, u32[]{:S(2)}) %all-to-all-start) | async-done | bytes 327712 | tf_op jit(solution)/shard_map/all_to_all | solution.py:48
  23.2 0.0 copy-start.3
  23.2 5.0 %fusion.35 = f32[320,3072]{1,0:T(8,128)} fusion(bf16[320,512]{1,0:T(8,128)(2,1)S(1)} %bitcast.36, bf16[512,3072]{0,1:T(8,128)(2,1)} %bitcast.34), kind=kOutput, calls=%fused_computation.57 | convolution fusion | flops 1006632960 | bytes 7405568 | tf_op jit(solution)/shard_map/dot_general | solution.py:53
  28.2 0.0 reduce-scatter.5.cloned.1.call-update
  28.2 0.0 all-gather.4.cloned.1.call-start
  28.3 0.7 all-gather.4.cloned.1.call-update
  29.0 0.0 all-gather.6.cloned.1.call-start
  29.0 0.0 copy-done.3
  29.1 7.2 %gather_fusion = bf16[40,64,1024]{2,1,0:T(8,128)(2,1)} fusion(bf16[40,64,1024]{2,1,0:T(8,128)(2,1)} %param.18, s32[1024]{0:T(1024)S(1)} %pad_clamp_fusion), kind=kCustom, calls=%fused_computation.clone | custom fusion | bytes 10485920 | tf_op jit(solution)/shard_map/jit(_take)/gather | solution.py:63
  36.3 7.6 %gather_fusion.1 = bf16[40,64,1024]{2,1,0:T(8,128)(2,1)} fusion(bf16[40,64,1024]{2,1,0:T(8,128)(2,1)} %param.19, s32[1024]{0:T(1024)S(1)} %pad_clamp_fusion), kind=kCustom, calls=%fused_computation.1.clone | custom fusion | bytes 10485920 | tf_op jit(solution)/shard_map/jit(_take)/gather | solution.py:66
  43.9 9.1 %broadcast_select_fusion.1 = (bf16[40,64,1024]{2,1,0:T(8,128)(2,1)}, bf16[40,64,1024]{2,1,0:T(8,128)(2,1)}) fusion(bf16[40,64,1024]{2,1,0:T(8,128)(2,1)} %gather_fusion, pred[40]{0:T(512)(128)(4,1)S(1)} %get-tuple-element.5, bf16[40,64,1024]{2,1,0:T(8,128)(2,1)} %gather_fusion.1), kind=kLoop, calls=%fused_computation.11 | loop fusion | flops 5242880 | bytes 20971560 | tf_op jit(solution)/shard_map/jit(_take)/select_n | solution.py:63
  52.9 24.6 %reduce-scatter.5.cloned.1.call-done = f32[40,3072]{1,0:T(8,128)} async-done(((f32[320,3072]{1,0:T(8,128)}), f32[40,3072]{1,0:T(8,128)}) %reduce-scatter.5.cloned.1.call-update) | async-done | bytes 491536 | tf_op jit(solution)/shard_map/reduce_scatter | solution.py:52
  77.6 1.1 convert_element_type.34
  78.6 0.4 reshape.54
  79.0 0.3 fusion.32
  79.3 11.1 %pad_maximum_fusion = (bf16[40,65,1024]{2,1,0:T(8,128)(2,1)}, bf16[40,65,1024]{2,1,0:T(8,128)(2,1)}) fusion(bf16[40,1,1024]{2,1,0:T(2,128)(2,1)S(1)} %get-tuple-element.7, bf16[40,64,1024]{2,1,0:T(8,128)(2,1)} %get-tuple-element.9, bf16[40,1,1024]{2,1,0:T(2,128)(2,1)S(1)} %get-tuple-element.8, bf16[40,64,1024]{2,1,0:T(8,128)(2,1)} %get-tuple-element.10), kind=kLoop, calls=%fused_computation.4 | loop fusion | flops 21299200 | bytes 21299200 | tf_op jit(solution)/shard_map/concatenate | solution.py:62
  90.4 9.1 %reshape.87 = bf16[40,65,8,128]{3,2,1,0:T(8,128)(2,1)} reshape(bf16[40,65,1024]{2,1,0:T(8,128)(2,1)} %get-tuple-element.11) | data formatting | bytes 10649600 | tf_op jit(solution)/shard_map/reshape | solution.py:68
  99.5 9.3 %reshape.88 = bf16[40,65,8,128]{3,2,1,0:T(8,128)(2,1)} reshape(bf16[40,65,1024]{2,1,0:T(8,128)(2,1)} %get-tuple-element.12) | data formatting | bytes 10649600 | tf_op jit(solution)/shard_map/reshape | solution.py:69
  108.8 5.9 %fusion.4 = f32[40,8,1,65]{3,2,1,0:T(1,128)S(1)} fusion(bf16[40,65,8,128]{3,2,1,0:T(8,128)(2,1)} %reshape.87, bf16[40,3,1024]{2,1,0:T(4,128)(2,1)S(1)} %reshape.54), kind=kOutput, calls=%fused_computation.8 | convolution fusion | flops 5324800 | bytes 5571840 | tf_op jit(solution)/shard_map/thd,tjhd->thj/dot_general | solution.py:71
  114.6 0.2 fusion.10
  114.9 4.2 %fusion.2 = f32[40,8,1,128]{3,2,1,0:T(1,128)S(1)} fusion(bf16[40,65,8,128]{3,2,1,0:T(8,128)(2,1)} %reshape.88, bf16[40,8,65,1]{2,1,0,3:T(8,128)(2,1)S(1)} %fusion.10), kind=kOutput, calls=%fused_computation.6 | convolution fusion | flops 5324800 | bytes 5530240 | tf_op jit(solution)/shard_map/thj,tjhd->thd/dot_general | solution.py:75
  119.1 16.2 %all-gather.4.cloned.1.call-done = bf16[1024,4096]{1,0:T(8,128)(2,1)} async-done(((bf16[1024,512]{1,0:T(8,128)(2,1)}), bf16[1024,4096]{1,0:T(8,128)(2,1)}) %all-gather.4.cloned.1.call-update) | async-done | bytes 8388624 | tf_op jit(solution)/shard_map/all_gather | solution.py:81
  135.3 5.9 %fusion.19 = f32[40,4096]{1,0:T(8,128)} fusion(bf16[1024,4096]{1,0:T(8,128)(2,1)} %all-gather.4.cloned.1.call-done, bf16[5,8,8,128]{3,2,1,0:T(8,128)(2,1)S(1)} %bitcast.38), kind=kOutput, calls=%fused_computation.34 | convolution fusion | flops 335544320 | bytes 9125888 | tf_op jit(solution)/shard_map/dot_general | solution.py:79
  141.2 0.0 all-gather.6.cloned.1.call-update
  141.2 0.0 reduce-scatter.7.cloned.1.call-start
  141.3 0.0 copy-done.2
  141.3 0.1 copy.31
  141.4 0.7 dynamic-slice
  142.1 54.1 %all-gather.6.cloned.1.call-done = f32[160,4096]{1,0:T(8,128)} async-done(((f32[40,4096]{1,0:T(8,128)}), f32[160,4096]{1,0:T(8,128)}) %all-gather.6.cloned.1.call-update) | async-done | bytes 2621456 | tf_op jit(solution)/shard_map/all_gather | solution.py:12
  196.1 2.8 %reduce_sum.38 = f32[40,4096]{1,0:T(8,128)} reduce(f32[4,40,4096]{2,1,0:T(8,128)} %bitcast.35, f32[]{:T(128)} %constant.20.clone.1), dimensions={0}, to_apply=%region_4.6 | reduce | flops 491520 | bytes 3276804 | tf_op jit(solution)/shard_map/reduce_sum | solution.py:12
  198.9 0.0 copy-done.1
  198.9 1.3 multiply_reduce_fusion
  200.2 0.0 copy-done
  200.2 0.5 convolution_bitcast_fusion
  200.8 0.3 convolution_convert_fusion
  201.2 0.7 copy.44
  201.9 0.0 reduce-scatter.7.cloned.1.call-update
  201.9 0.8 convert_element_type.37
  202.7 17.5 %reduce-scatter.7.cloned.1.call-done = bf16[64,40]{1,0:T(8,128)(2,1)} async-done(((bf16[256,40]{1,0:T(8,128)(2,1)}), bf16[64,40]{1,0:T(8,128)(2,1)}) %reduce-scatter.7.cloned.1.call-update) | async-done | bytes 5136
  220.1 0.8 copy.43
  220.9 0.6 convert_element_type.41
  (8 shorter events, 0.1 us)
Async XLA Ops:
  7.2 193.1 %copy-start = (bf16[1024,1024]{1,0:T(8,128)(2,1)S(1)}, bf16[1024,1024]{1,0:T(8,128)(2,1)}, u32[]{:S(2)}) copy-start(bf16[1024,1024]{1,0:T(8,128)(2,1)} %param.17) | copy-start | bytes 6291460
  10.4 12.8 %all-to-all-start = ((bf16[40,8,512]{2,0,1:T(8,128)(2,1)}), bf16[40,8,512]{2,0,1:T(8,128)(2,1)S(1)}, u32[]{:S(2)}, u32[]{:S(2)}) async-start(bf16[40,8,512]{2,0,1:T(8,128)(2,1)} %bitcast.33), calls=%async_computation | async-start | bytes 655360 | tf_op jit(solution)/shard_map/all_to_all | solution.py:48
  15.6 62.0 %reduce-scatter.5.cloned.1.call-start = ((), (), s32[]{:S(2)}) async-start(), calls=%async_computation.3 | async-start | bytes 4423680 | tf_op jit(solution)/shard_map/reduce_scatter | solution.py:52
  23.2 5.8 %copy-start.3 = (s32[40]{0:T(128)S(1)}, s32[40]{0:T(128)}, u32[]{:S(2)}) copy-start(s32[40]{0:T(128)} %param.20) | copy-start | bytes 484
  28.2 107.1 %all-gather.4.cloned.1.call-start = ((), (), s32[]{:S(2)}) async-start(), calls=%async_computation.4 | async-start | bytes 9437184 | tf_op jit(solution)/shard_map/all_gather | solution.py:81
  29.0 167.2 %all-gather.6.cloned.1.call-start = ((), (), s32[]{:S(2)}) async-start(), calls=%async_computation.5 | async-start | bytes 3276800 | tf_op jit(solution)/shard_map/all_gather | solution.py:12
  135.3 6.0 %copy-start.2 = (s32[40,2]{0,1:T(2,128)S(1)}, s32[40,2]{0,1:T(2,128)}, u32[]{:S(2)}) copy-start(s32[40,2]{0,1:T(2,128)} %param.21) | copy-start | bytes 964
  135.3 63.6 %copy-start.1 = (bf16[40,4096]{1,0:T(8,128)(2,1)S(1)}, bf16[40,4096]{1,0:T(8,128)(2,1)}, u32[]{:S(2)}) copy-start(bf16[40,4096]{1,0:T(8,128)(2,1)} %param.12) | copy-start | bytes 983044
  141.2 78.9 %reduce-scatter.7.cloned.1.call-start = ((), (), s32[]{:S(2)}) async-start(), calls=%async_computation.6 | async-start | bytes 81920
Sparse Core Ops, SparseCore 0:
  28.3 49.1 reduce-scatter.4
  79.4 55.8 all-gather.3
  141.4 54.7 all-gather.5
  202.0 18.0 reduce-scatter.6
